TPU v7x, 32 devices: a whole 2x2x4 slice. The times are simulated.
32 devices in a mesh: slab: 4 (over y, core), inner: 8 (over z, x).
Axes of the slice: x: 2, y: 2, z: 4, core: 2. Of those that a mesh axis runs over, the one named last changes fastest.
Arguments:
- x_in: bfloat16 [8192, 16384], P(('slab', 'inner')), may hold values from -6 to 6
- bc_in: bfloat16 [8192, 4096], P(('slab', 'inner')), may hold values from -6 to 6
- dt_raw: bfloat16 [8192, 256], P(('slab', 'inner')), may hold values from -6.7 to -4.3
- dt_bias: float32 [256], replicated, may hold values from -0.5 to 0.5
- a_log: float32 [256], replicated, may hold values from -8 to 0, as said below
- d_skip: float32 [256], replicated, may hold values from 0.5 to 1.5
- conv_x_weight: float32 [4, 16384], replicated, may hold values from -3 to 3
- conv_x_bias: float32 [16384], replicated, may hold values from -3 to 3
- conv_bc_weight: float32 [4, 4096], replicated, may hold values from -3 to 3
- conv_bc_bias: float32 [4096], replicated, may hold values from -3 to 3
Outputs:
- y_out: bfloat16 [8192, 16384], P('slab', 'inner')
Inputs may be any that keep to these rules, and one draw needn't show every extreme that they name: `a_log`: per-head logarithm of the decay rate.
All inputs are finite; a program needn't handle non-finite values.
Results may differ from a plain program's by a relative error of at most 0.0034.
Values may be sent and summed in bfloat16 or wider, within the bound.
No kernel may reach another device: no remote copies, remote signals or barrier semaphores. Data moves between devices by JAX's collectives and lax.ppermute only.
A program may use at most 256 MiB of HBM per device.

v0:
```python
import jax
import jax.numpy as jnp
import numpy as np
from jax import lax
from jax.sharding import PartitionSpec as P

HEADS = 256
HEADDIM = 64
STATE = 256
GROUPS = 8
CONV = 4
SPAN = 256


def from_behind(x, axis, by):
    size = lax.axis_size(axis)
    pairs = [(i, i + by) for i in range(size) if 0 <= i + by < size]
    return lax.ppermute(x, axis, pairs)


def causal_conv(row_block, before, weight, conv_bias):
    kernel_len = weight.shape[0]
    length = row_block.shape[0]
    padded = jnp.concatenate([before, row_block], axis=0).astype(jnp.float32)
    summed = conv_bias[None, :] + weight[0][None, :] * padded[0:length]
    for offset in range(1, kernel_len):
        summed = summed + weight[offset][None, :] * padded[offset : offset + length]
    return jax.nn.silu(summed).astype(jnp.bfloat16)


def head_columns(per_head, head_count):
    rows = per_head.shape[0]
    return jnp.broadcast_to(per_head[:, :, None], (rows, head_count, HEADDIM)).reshape(
        rows, head_count * HEADDIM
    )


def span_step(state, pieces):
    x_span, b_span, c_span, dt_span, da_span = pieces
    size_q = x_span.shape[0]
    head_count = dt_span.shape[1]
    cumul = jnp.cumsum(da_span, axis=0).T
    row_ids = lax.broadcasted_iota(jnp.int32, (size_q, size_q), 0)
    col_ids = lax.broadcasted_iota(jnp.int32, (size_q, size_q), 1)
    gaps = cumul[:, :, None] - cumul[:, None, :]
    decays = jnp.where((row_ids >= col_ids)[None], jnp.exp(jnp.minimum(gaps, 0.0)), 0.0)
    scores = jnp.dot(c_span, b_span.T, preferred_element_type=jnp.float32)
    mixing = (decays * scores[None] * dt_span.T[:, None, :]).astype(jnp.bfloat16)
    x_heads = x_span.reshape(size_q, head_count, HEADDIM)
    y_intra = jnp.einsum(
        "hts,shp->thp", mixing, x_heads, preferred_element_type=jnp.float32
    ).reshape(size_q, head_count * HEADDIM)
    y_inter = jnp.dot(c_span, state.astype(jnp.bfloat16), preferred_element_type=jnp.float32)
    y_inter = y_inter * head_columns(jnp.exp(cumul.T), head_count)
    weights_end = (jnp.exp(cumul[:, -1:] - cumul) * dt_span.T).T
    scaled = (x_span.astype(jnp.float32) * head_columns(weights_end, head_count)).astype(
        jnp.bfloat16
    )
    contrib = jnp.dot(b_span.T, scaled, preferred_element_type=jnp.float32)
    end_decay = head_columns(jnp.exp(cumul[:, -1])[None, :], head_count)
    new_state = end_decay * state + contrib
    return (new_state, y_intra + y_inter)


def slab_core(x_rows, b_rows, c_rows, dt_rows, da_rows):
    length = x_rows.shape[0]
    width = x_rows.shape[1]
    head_count = dt_rows.shape[1]
    span_count = length // SPAN
    inputs = (
        x_rows.reshape(span_count, SPAN, width),
        b_rows.reshape(span_count, SPAN, STATE),
        c_rows.reshape(span_count, SPAN, STATE),
        dt_rows.reshape(span_count, SPAN, head_count),
        da_rows.reshape(span_count, SPAN, head_count),
    )
    zero_state = jnp.zeros((STATE, width), jnp.float32)
    end_state, outputs = lax.scan(span_step, zero_state, inputs)
    return (outputs.reshape(length, width), end_state)


def group_copies(bc_rows, dest_group, n_inner):
    tok_rows = bc_rows.shape[0]
    split = bc_rows.reshape(tok_rows, 2, GROUPS, STATE)
    picked = jnp.take(split, dest_group, axis=2)
    return jnp.transpose(picked, (0, 2, 1, 3)).reshape(tok_rows, n_inner, 2 * STATE)


def shards(
    x_in,
    bc_in,
    dt_raw,
    dt_bias,
    a_log,
    d_skip,
    conv_x_weight,
    conv_x_bias,
    conv_bc_weight,
    conv_bc_bias,
):
    n_inner = lax.axis_size("inner")
    n_slab = lax.axis_size("slab")
    tok_dev = x_in.shape[0]
    heads_dev = HEADS // n_inner
    ch_dev = heads_dev * HEADDIM
    per_group = HEADS // GROUPS
    inner_idx = lax.axis_index("inner")
    dest_group = np.arange(n_inner) * heads_dev // per_group
    edge = CONV - 1
    dt_send = dt_raw.reshape(tok_dev, n_inner, heads_dev)
    x_prev, bc_prev = from_behind(
        (x_in[tok_dev - edge :], bc_in[tok_dev - edge :]), ("slab", "inner"), 1
    )
    x_ready = causal_conv(x_in, x_prev, conv_x_weight, conv_x_bias)
    bc_ready = causal_conv(bc_in, bc_prev, conv_bc_weight, conv_bc_bias)
    bc_send = group_copies(bc_ready, dest_group, n_inner)
    x_recv, bc_recv, dt_recv = (
        lax.all_to_all(
            x_ready.reshape(tok_dev, n_inner, ch_dev),
            "inner",
            split_axis=1,
            concat_axis=0,
            tiled=True,
        ),
        lax.all_to_all(bc_send, "inner", split_axis=1, concat_axis=0, tiled=True),
        lax.all_to_all(dt_send, "inner", split_axis=1, concat_axis=0, tiled=True),
    )
    x_slab = x_recv.reshape(-1, ch_dev)
    bc_slab = bc_recv.reshape(-1, 2 * STATE)
    bias_heads = lax.dynamic_slice_in_dim(dt_bias, inner_idx * heads_dev, heads_dev, 0)
    rate_heads = -jnp.exp(lax.dynamic_slice_in_dim(a_log, inner_idx * heads_dev, heads_dev, 0))
    skip_heads = lax.dynamic_slice_in_dim(d_skip, inner_idx * heads_dev, heads_dev, 0)
    dt_heads = jax.nn.softplus(
        dt_recv.reshape(-1, heads_dev).astype(jnp.float32) + bias_heads[None, :]
    )
    da_heads = dt_heads * rate_heads[None, :]
    c_slab = bc_slab[:, STATE:]
    y_local, end_state = slab_core(x_slab, bc_slab[:, :STATE], c_slab, dt_heads, da_heads)
    cum_slab = jnp.cumsum(da_heads, axis=0)
    slab_decay = head_columns(jnp.exp(cum_slab[-1:]), heads_dev)[0]
    incoming = jnp.zeros_like(end_state)
    outgoing = end_state
    for hop_number in range(n_slab - 1):
        incoming = from_behind(outgoing, "slab", 1)
        outgoing = slab_decay[None, :] * incoming + end_state
    carried = jnp.dot(c_slab, incoming.astype(jnp.bfloat16), preferred_element_type=jnp.float32)
    carried = carried * head_columns(jnp.exp(cum_slab), heads_dev)
    skip_cols = jnp.repeat(skip_heads, HEADDIM)
    y_slab = y_local + carried + skip_cols[None, :] * x_slab.astype(jnp.float32)
    return y_slab.astype(jnp.bfloat16)


def solution(mesh):
    placed = (
        P(("slab", "inner"), None),
        P(("slab", "inner"), None),
        P(("slab", "inner"), None),
        P(),
        P(),
        P(),
        P(),
        P(),
        P(),
        P(),
    )
    return jax.shard_map(
        shards, mesh=mesh, in_specs=placed, out_specs=P("slab", "inner"), check_vma=False
    )
```

profile of v0, /device:TPU:0, one launch (start us, length us, event | category | flops | bytes accessed | tf_op | source)
XLA Modules:
  0.0 606.8 jit_solution(15291614099124217635)
XLA Ops:
  1.7 7.3 %all-to-all-start = ((bf16[256,8,32]{0,2,1:T(8,128)(2,1)}), bf16[256,8,32]{0,2,1:T(8,128)(2,1)S(1)}, u32[]{:S(2)}, u32[]{:S(2)}) async-start(bf16[256,8,32]{0,2,1:T(8,128)(2,1)} %bitcast), calls=%async_computation | async-start | bytes 262144 | tf_op jit(solution)/shard_map/all_to_all | solution.py:126
  9.8 4.5 collective-permute-start
  16.0 3.4 collective-permute-start.1
  23.8 3.3 copy.92
  29.7 7.0 %multiply_convert_fusion.4 = bf16[256,4096]{0,1:T(8,128)(2,1)S(1)} fusion(f32[259,4096]{0,1:T(8,128)S(1)} %maximum_convert_fusion.1, f32[4096]{0:T(1024)S(1)} %bitcast.210, f32[4096]{0:T(1024)S(1)} %bitcast.211, f32[4096]{0:T(1024)S(1)} %bitcast.209, f32[4096]{0:T(1024)S(1)} %bitcast.208, f32[4096]{0:T(1024)S(1)} %copy-done.6), kind=kLoop, calls=%fused_computation.66 | loop fusion | flops 13631488 | bytes 18956288 | tf_op jit(solution)/shard_map/convert_element_type | solution.py:28
  43.1 3.9 copy.94
  47.0 11.8 %maximum_convert_fusion = f32[259,16384]{1,0:T(8,128)} fusion(bf16[256,16384]{1,0:T(8,128)(2,1)} %param.13, bf16[3,16384]{1,0:T(4,128)(2,1)} %collective-permute-done.1), kind=kLoop, calls=%fused_computation.56 | loop fusion | flops 16973824 | bytes 25460736 | tf_op jit(solution)/shard_map/convert_element_type | solution.py:24
  58.8 4.0 all-to-all-start.1
  62.8 27.1 %multiply_convert_fusion.3 = bf16[256,16384]{1,0:T(8,128)(2,1)} fusion(f32[259,16384]{1,0:T(8,128)} %maximum_convert_fusion, f32[16384]{0:T(1024)S(1)} %bitcast.204, f32[16384]{0:T(1024)S(1)} %bitcast.205, f32[16384]{0:T(1024)S(1)} %bitcast.203, f32[16384]{0:T(1024)S(1)} %bitcast.202, f32[16384]{0:T(1024)S(1)} %copy-done.5), kind=kLoop, calls=%fused_computation.55 | loop fusion | flops 54525952 | bytes 75825152 | tf_op jit(solution)/shard_map/convert_element_type | solution.py:28
  89.9 11.9 %copy.96 = bf16[256,16384]{0,1:T(8,128)(2,1)} copy(bf16[256,16384]{1,0:T(8,128)(2,1)} %multiply_convert_fusion.3) | data formatting | bytes 16777216 | tf_op jit(solution)/shard_map/convert_element_type | solution.py:28
  101.9 10.6 %all-to-all-done.1 = bf16[256,8,512]{0,2,1:T(8,128)(2,1)S(1)} async-done(((bf16[256,8,512]{0,2,1:T(8,128)(2,1)}), bf16[256,8,512]{0,2,1:T(8,128)(2,1)S(1)}, u32[]{:S(2)}, u32[]{:S(2)}) %all-to-all-start.1) | async-done | bytes 2097184 | tf_op jit(solution)/shard_map/all_to_all | solution.py:125
  113.7 5.1 all-to-all-start.2
  120.1 3.9 copy.95
  124.0 3.0 fusion.49
  127.1 175.1 %all-to-all-done.2 = bf16[256,8,2048]{0,2,1:T(8,128)(2,1)} async-done(((bf16[256,8,2048]{0,2,1:T(8,128)(2,1)}), bf16[256,8,2048]{0,2,1:T(8,128)(2,1)}, u32[]{:S(2)}, u32[]{:S(2)}) %all-to-all-start.2) | async-done | bytes 8388640 | tf_op jit(solution)/shard_map/all_to_all | solution.py:118
  302.1 194.8 %while.13 = (s32[]{:T(128)}, f32[256,2048]{1,0:T(8,128)S(1)}, f32[8,256,2048]{2,1,0:T(8,128)}, f32[8,256,32]{1,2,0:T(8,128)}, bf16[8,256,256]{2,1,0:T(8,128)(2,1...) while((s32[]{:T(128)}, f32[256,2048]{1,0:T(8,128)S(1)}, ...), condition=%wide.region_3.4_spmd.clone, body=%wide.region_0.3_spmd.clone.sunk | while | flops 857301120 | bytes 33167368 | solution.py:78
  307.3 4.2 fusion.72
  311.5 2.9 copy.127
  318.8 4.1 fusion.73
  331.7 4.2 fusion.72
  335.9 2.9 copy.127
  343.2 4.0 fusion.73
  356.0 4.2 fusion.72
  360.2 2.9 copy.127
  367.5 4.0 fusion.73
  380.4 4.2 fusion.72
  384.5 2.9 copy.127
  391.9 4.1 fusion.73
  404.7 4.2 fusion.72
  408.9 2.9 copy.127
  416.2 4.1 fusion.73
  429.1 4.2 fusion.72
  433.3 2.9 copy.127
  440.6 4.0 fusion.73
  453.4 4.2 fusion.72
  465.0 4.0 fusion.73
  477.8 4.2 fusion.72
  482.0 2.9 copy.127
  489.3 4.0 fusion.73
  499.9 9.1 %reduce-window.16 = f32[32,16,128]{2,1,0:T(8,128)S(1)} reduce-window(f32[32,16,128]{2,1,0:T(8,128)S(1)} %bitcast.199, f32[]{:T(128)} %constant.44.clone.1), window={size=1x1x128 pad=0_0x0_0x127_0}, to_apply=%region_4.5 | reduce-window | flops 8323072 | bytes 524292 | tf_op jit(solution)/shard_map/reduce-window.2
  510.1 3.3 multiply_add_fusion.1
  513.4 14.0 %collective-permute-start.3 = (f32[256,2048]{1,0:T(8,128)}, f32[256,2048]{1,0:T(8,128)}, u32[]{:S(2)}, u32[]{:S(2)}) collective-permute-start(f32[256,2048]{1,0:T(8,128)} %multiply_add_fusion.1), channel_id=1, source_target_pairs={{0,8},{8,16},{16,24},{1,9},{9,17},{17,25},{2,10},{10,18},{18,26},{... | collective-permute-start | bytes 6291464 | tf_op jit(solution)/shard_map/ppermute | solution.py:18
  527.7 7.8 %broadcast_in_dim.88 = f32[2048,32,64]{0,2,1:T(8,128)} broadcast(f32[2048,32]{0,1:T(8,128)S(1)} %fusion.47), dimensions={0,1} | broadcast | bytes 17039360 | tf_op jit(solution)/shard_map/broadcast_in_dim | solution.py:33
  535.6 17.6 %copy.100 = f32[2048,2048]{1,0:T(8,128)} copy(f32[2048,2048]{0,1:T(8,128)} %bitcast.189) | data formatting | bytes 33554432 | tf_op jit(solution)/shard_map/reshape | solution.py:33
  556.1 3.2 collective-permute-start.4
  559.3 10.6 %bitcast_convert_fusion = f32[8,256,1,2048]{1,3,0,2:T(8,128)} fusion(bf16[256,8,2048]{0,2,1:T(8,128)(2,1)} %all-to-all-done.2), kind=kLoop, calls=%fused_computation.57 | loop fusion | flops 4194304 | bytes 25165824 | tf_op jit(solution)/shard_map/convert_element_type | solution.py:149
  569.9 16.6 %copy.101 = f32[8,256,1,2048]{3,1,0,2:T(8,128)} copy(f32[8,256,1,2048]{1,3,0,2:T(8,128)} %bitcast_convert_fusion) | data formatting | bytes 33554432 | tf_op jit(solution)/shard_map/convert_element_type | solution.py:149
  586.5 20.3 %fusion.31 = bf16[2048,2048]{1,0:T(8,128)(2,1)} fusion(f32[8,256,1,2048]{3,1,0,2:T(8,128)} %copy.101, f32[8,256,2048]{2,1,0:T(8,128)} %get-tuple-element.48, f32[2048,2048]{1,0:T(8,128)} %copy.100, f32[2048]{0:T(1024)S(1)} %mul.208, bf16[256,2048]{1,0:T(8,128)(2,1)S(1)} %collective-permute-done.4, bf16[2048,512]{1,0:T(8,128)(2,1)S(1)} %bitcast.193), kind=kOutput, calls=%fused_computation.53 | convolution fusion | flops 2168455168 | bytes 60825600 | tf_op jit(solution)/shard_map/dot_general | solution.py:146
  (209 shorter events, 135.1 us)
Async XLA Ops:
  1.7 57.1 %all-to-all-start = ((bf16[256,8,32]{0,2,1:T(8,128)(2,1)}), bf16[256,8,32]{0,2,1:T(8,128)(2,1)S(1)}, u32[]{:S(2)}, u32[]{:S(2)}) async-start(bf16[256,8,32]{0,2,1:T(8,128)(2,1)} %bitcast), calls=%async_computation | async-start | bytes 262144 | tf_op jit(solution)/shard_map/all_to_all | solution.py:126
  9.8 17.2 %collective-permute-start = (bf16[3,4096]{1,0:T(4,128)(2,1)S(1)}, bf16[3,4096]{1,0:T(4,128)(2,1)}, u32[]{:S(2)}, u32[]{:S(2)}) collective-permute-start(bf16[3,4096]{1,0:T(4,128)(2,1)S(1)} %slice.80), channel_id=1, source_target_pairs={{0,1},{1,2},{2,3},{3,4},{4,5},{5,6},{6,7},{7,8},{8,9},{9,10},{10,1... | collective-permute-start | bytes 73736 | tf_op jit(solution)/shard_map/ppermute | solution.py:18
  16.0 31.0 %collective-permute-start.1 = (bf16[3,16384]{1,0:T(4,128)(2,1)}, bf16[3,16384]{1,0:T(4,128)(2,1)}, u32[]{:S(2)}, u32[]{:S(2)}) collective-permute-start(bf16[3,16384]{1,0:T(4,128)(2,1)} %slice.90), channel_id=1, source_target_pairs={{0,1},{1,2},{2,3},{3,4},{4,5},{5,6},{6,7},{7,8},{8,9},{9,10},{10,1... | collective-permute-start | bytes 294920 | tf_op jit(solution)/shard_map/ppermute | solution.py:18
  28.3 1.4 copy-start.2
  28.3 1.4 copy-start.3
  28.3 1.4 copy-start.4
  28.3 1.4 copy-start.6
  36.7 4.8 copy-start.7
  58.8 4.0 copy-start.5
  58.8 53.6 %all-to-all-start.1 = ((bf16[256,8,512]{0,2,1:T(8,128)(2,1)}), bf16[256,8,512]{0,2,1:T(8,128)(2,1)S(1)}, u32[]{:S(2)}, u32[]{:S(2)}) async-start(bf16[256,8,512]{0,2,1:T(8,128)(2,1)} %bitcast.195), calls=%async_computation.1 | async-start | bytes 4194304 | tf_op jit(solution)/shard_map/all_to_all | solution.py:125
  112.4 1.3 copy-start.1
  112.4 6.5 %copy-start.8 = (f32[256]{0:T(256)S(1)}, f32[256]{0:T(256)}, u32[]{:S(2)}) copy-start(f32[256]{0:T(256)} %param.16) | copy-start | bytes 3076
  112.4 6.6 %copy-start.9 = (f32[256]{0:T(256)S(1)}, f32[256]{0:T(256)}, u32[]{:S(2)}) copy-start(f32[256]{0:T(256)} %param.17) | copy-start | bytes 3076
  113.7 188.4 %all-to-all-start.2 = ((bf16[256,8,2048]{0,2,1:T(8,128)(2,1)}), bf16[256,8,2048]{0,2,1:T(8,128)(2,1)}, u32[]{:S(2)}, u32[]{:S(2)}) async-start(bf16[256,8,2048]{0,2,1:T(8,128)(2,1)} %bitcast.191), calls=%async_computation.2 | async-start | bytes 16777216 | tf_op jit(solution)/shard_map/all_to_all | solution.py:118
  496.9 13.2 %collective-permute-start.2 = (f32[256,2048]{1,0:T(8,128)S(1)}, f32[256,2048]{1,0:T(8,128)}, u32[]{:S(2)}, u32[]{:S(2)}) collective-permute-start(f32[256,2048]{1,0:T(8,128)S(1)} %get-tuple-element.49), channel_id=1, source_target_pairs={{0,8},{8,16},{16,24},{1,9},{9,17},{17,25},{2,10},{10,18},{18,26},{... | collective-permute-start | bytes 6291464 | tf_op jit(solution)/shard_map/ppermute | solution.py:18
  509.0 18.4 %copy-start.10 = (f32[256]{0:T(256)S(1)}, f32[256]{0:T(256)}, u32[]{:S(2)}) copy-start(f32[256]{0:T(256)} %param.18) | copy-start | bytes 3076
  513.4 39.8 %collective-permute-start.3 = (f32[256,2048]{1,0:T(8,128)}, f32[256,2048]{1,0:T(8,128)}, u32[]{:S(2)}, u32[]{:S(2)}) collective-permute-start(f32[256,2048]{1,0:T(8,128)} %multiply_add_fusion.1), channel_id=1, source_target_pairs={{0,8},{8,16},{16,24},{1,9},{9,17},{17,25},{2,10},{10,18},{18,26},{... | collective-permute-start | bytes 6291464 | tf_op jit(solution)/shard_map/ppermute | solution.py:18
  556.1 30.4 %collective-permute-start.4 = (bf16[256,2048]{1,0:T(8,128)(2,1)}, bf16[256,2048]{1,0:T(8,128)(2,1)S(1)}, u32[]{:S(2)}, u32[]{:S(2)}) collective-permute-start(bf16[256,2048]{1,0:T(8,128)(2,1)} %multiply_add_fusion), channel_id=1, source_target_pairs={{0,8},{8,16},{16,24},{1,9},{9,17},{17,25},{2,10},{10,18},{18,26},{... | collective-permute-start | bytes 3145736 | tf_op jit(solution)/shard_map/ppermute | solution.py:18
  569.9 16.6 %copy-start = (bf16[8,256,1,512]{3,1,0,2:T(8,128)(2,1)S(1)}, bf16[8,256,1,512]{3,1,0,2:T(8,128)(2,1)}, u32[]{:S(2)}) copy-start(bf16[8,256,1,512]{3,1,0,2:T(8,128)(2,1)} %copy.95) | copy-start | bytes 6291460
where the time goes:
time: 611 us; the launch traced here: 607 us
  waiting for transfers between devices  186 us (30%)
  local copies, waits for them, and re-layouts  163 us (27%)
  matrix products  113 us (18%)
  other arithmetic  99.8 us (16%)
  starting transfers between devices  44.3 us (7%)
    all_to_all x1, waiting for transfers between devices, shards(): lax.all_to_all(x_ready.reshape(tok_dev, n_inner, ch_dev), 'inner', split_...  175 us
    reshape x9, local copies, waits for them, and re-layouts, head_columns(): jnp.broadcast_to(per_head[:, :, None], (rows, head_count, HEADDIM))  40.8 us
    convert_element_type x2, other arithmetic, causal_conv(): return jax.nn.silu(summed).astype(jnp.bfloat16)  34.1 us
    dot_general x8, matrix products, span_step(): jnp.einsum('hts,shp->thp', mixing, x_heads, preferred_element_type=jnp.fl...  33.6 us
    dot_general x8, matrix products, span_step(): jnp.dot(c_span, state.astype(jnp.bfloat16), preferred_element_type=jnp.fl...  32.4 us
    ppermute x5, starting transfers between devices, from_behind(): return lax.ppermute(x, axis, pairs)  27.8 us
    reshape x8, local copies, waits for them, and re-layouts, span_step(): y_intra = jnp.einsum('hts,shp->thp', mixing, x_heads, preferred_element_t...  23.5 us
    broadcast_in_dim x27, local copies, waits for them, and re-layouts, head_columns(): jnp.broadcast_to(per_head[:, :, None], (rows, head_count, HEADDIM))  21 us
  transfers between devices with their start and end apart: 8, of which 2 were waited for; matrix products, arithmetic and copies ran while one was open for 25% of the time, Pallas kernels for 0%

commit v1 on v0

--- a/solution.py
+++ b/solution.py
@@ -10,6 +10,22 @@
 GROUPS = 8
 CONV = 4
 SPAN = 256
+
+
+def swapped_with_each(array, axis, split, join):
+    ways, here = (lax.axis_size(axis), lax.axis_index(axis))
+    width = array.shape[split] // ways
+    shape = list(array.shape)
+    shape[split] = width
+    height = shape[join]
+    shape[join] = height * ways
+    full = jnp.zeros(shape, array.dtype)
+    for mask in range(ways):
+        part = lax.dynamic_slice_in_dim(array, (here ^ mask) * width, width, axis=split)
+        if mask:
+            part = lax.ppermute(part, axis, [(d, d ^ mask) for d in range(ways)])
+        full = lax.dynamic_update_slice_in_dim(full, part, (here ^ mask) * height, axis=join)
+    return full
 
 
 def from_behind(x, axis, by):
@@ -115,13 +131,7 @@
     bc_ready = causal_conv(bc_in, bc_prev, conv_bc_weight, conv_bc_bias)
     bc_send = group_copies(bc_ready, dest_group, n_inner)
     x_recv, bc_recv, dt_recv = (
-        lax.all_to_all(
-            x_ready.reshape(tok_dev, n_inner, ch_dev),
-            "inner",
-            split_axis=1,
-            concat_axis=0,
-            tiled=True,
-        ),
+        swapped_with_each(x_ready.reshape(tok_dev, n_inner, ch_dev), "inner", 1, 0),
         lax.all_to_all(bc_send, "inner", split_axis=1, concat_axis=0, tiled=True),
         lax.all_to_all(dt_send, "inner", split_axis=1, concat_axis=0, tiled=True),
     )

time: 611 us -> 652 us (1.067)
  the two profiles are of different devices: /device:TPU:0 before, /device:TPU:17 now
where the time goes in v1:
time: 652 us; the launch traced here: 648 us
  local copies, waits for them, and re-layouts  210 us (32%)
  waiting for transfers between devices  188 us (29%)
  matrix products  112 us (17%)
  other arithmetic  101 us (15%)
  starting transfers between devices  36.3 us (6%)
    ppermute x7, waiting for transfers between devices, swapped_with_each(): part = lax.ppermute(part, axis, [(d, d ^ mask) for d in range(ways)])  154 us
    convert_element_type x2, other arithmetic, causal_conv(): return jax.nn.silu(summed).astype(jnp.bfloat16)  44.9 us
    reshape x9, local copies, waits for them, and re-layouts, head_columns(): jnp.broadcast_to(per_head[:, :, None], (rows, head_count, HEADDIM))  41 us
    ppermute x5, waiting for transfers between devices, from_behind(): return lax.ppermute(x, axis, pairs)  34.2 us
    dot_general x8, matrix products, span_step(): jnp.einsum('hts,shp->thp', mixing, x_heads, preferred_element_type=jnp.fl...  33.4 us
    unnamed x38, local copies, waits for them, and re-layouts  32.7 us
    dot_general x8, matrix products, span_step(): jnp.dot(c_span, state.astype(jnp.bfloat16), preferred_element_type=jnp.fl...  32.4 us
    dynamic_slice x16, local copies, waits for them, and re-layouts, slab_core(): end_state, outputs = lax.scan(span_step, zero_state, inputs)  30.4 us
  transfers between devices with their start and end apart: 14, of which 7 were waited for; matrix products, arithmetic and copies ran while one was open for 27% of the time, Pallas kernels for 0%

profile of v1, /device:TPU:17, one launch (start us, length us, event | category | flops | bytes accessed | tf_op | source)
XLA Modules:
  0.0 648.0 jit_solution(498487599189432252)
XLA Ops:
  1.7 3.1 collective-permute-start.1
  6.5 5.8 all-to-all-start
  13.1 3.1 collective-permute-start
  20.6 11.9 %copy.132 = bf16[256,16384]{0,1:T(8,128)(2,1)} copy(bf16[256,16384]{1,0:T(8,128)(2,1)} %param.13) | data formatting | bytes 16777216 | tf_op args[0]
  32.5 3.3 copy.127
  38.5 7.0 %multiply_convert_fusion.4 = bf16[256,4096]{0,1:T(8,128)(2,1)S(1)} fusion(f32[259,4096]{0,1:T(8,128)S(1)} %maximum_convert_fusion.1, f32[4096]{0:T(1024)S(1)} %bitcast.202, f32[4096]{0:T(1024)S(1)} %bitcast.203, f32[4096]{0:T(1024)S(1)} %bitcast.201, f32[4096]{0:T(1024)S(1)} %bitcast.200, f32[4096]{0:T(1024)S(1)} %copy-done.7), kind=kLoop, calls=%fused_computation.65 | loop fusion | flops 13631488 | bytes 18956288 | tf_op jit(solution)/shard_map/convert_element_type | solution.py:44
  52.0 3.9 copy.129
  55.9 4.1 copy.131
  60.0 14.8 %maximum_convert_fusion = f32[259,16384]{0,1:T(8,128)} fusion(bf16[256,16384]{0,1:T(8,128)(2,1)} %copy.132, bf16[3,16384]{0,1:T(8,128)(2,1)} %copy.131), kind=kLoop, calls=%fused_computation.56 | loop fusion | flops 16973824 | bytes 25460736 | tf_op jit(solution)/shard_map/convert_element_type | solution.py:40
  74.8 5.2 all-to-all-start.1
  80.0 37.9 %multiply_convert_fusion.3 = bf16[256,16384]{0,1:T(8,128)(2,1)} fusion(f32[259,16384]{0,1:T(8,128)} %maximum_convert_fusion, f32[16384]{0:T(1024)S(1)} %bitcast.196, f32[16384]{0:T(1024)S(1)} %bitcast.197, f32[16384]{0:T(1024)S(1)} %bitcast.195, f32[16384]{0:T(1024)S(1)} %bitcast.194, f32[16384]{0:T(1024)S(1)} %copy-done.6), kind=kLoop, calls=%fused_computation.55 | loop fusion | flops 54525952 | bytes 75825152 | tf_op jit(solution)/shard_map/convert_element_type | solution.py:44
  117.9 5.8 constant_dynamic-slice_fusion.1
  138.6 3.3 collective-permute-start.6
  141.8 4.5 broadcast_in_dim.88
  154.7 33.3 %collective-permute-done.3 = bf16[256,1,2048]{2,0,1:T(8,128)(2,1)} collective-permute-done((bf16[256,1,2048]{2,0,1:T(8,128)(2,1)}, bf16[256,1,2048]{2,0,1:T(8,128)(2,1)}, u32[]{:S(2)}, u32[]{:S(2)}) %collective-permute-start.3) | collective-permute-done | bytes 1048608 | tf_op jit(solution)/shard_map/ppermute | solution.py:26
  190.3 20.1 %collective-permute-done.4 = bf16[256,1,2048]{2,0,1:T(8,128)(2,1)} collective-permute-done((bf16[256,1,2048]{2,0,1:T(8,128)(2,1)}, bf16[256,1,2048]{2,0,1:T(8,128)(2,1)}, u32[]{:S(2)}, u32[]{:S(2)}) %collective-permute-start.4) | collective-permute-done | bytes 1048608 | tf_op jit(solution)/shard_map/ppermute | solution.py:26
  215.0 54.8 %collective-permute-done.6 = bf16[256,1,2048]{2,0,1:T(8,128)(2,1)} collective-permute-done((bf16[256,1,2048]{2,0,1:T(8,128)(2,1)}, bf16[256,1,2048]{2,0,1:T(8,128)(2,1)}, u32[]{:S(2)}, u32[]{:S(2)}) %collective-permute-start.6) | collective-permute-done | bytes 1048608 | tf_op jit(solution)/shard_map/ppermute | solution.py:26
  272.1 23.2 %collective-permute-done.7 = bf16[256,1,2048]{2,0,1:T(8,128)(2,1)S(1)} collective-permute-done((bf16[256,1,2048]{2,0,1:T(8,128)(2,1)}, bf16[256,1,2048]{2,0,1:T(8,128)(2,1)S(1)}, u32[]{:S(2)}, u32[]{:S(2)}) %collective-permute-start.7) | collective-permute-done | bytes 1048608 | tf_op jit(solution)/shard_map/ppermute | solution.py:26
  296.3 22.3 %collective-permute-done.8 = bf16[256,1,2048]{2,0,1:T(8,128)(2,1)S(1)} collective-permute-done((bf16[256,1,2048]{2,0,1:T(8,128)(2,1)}, bf16[256,1,2048]{2,0,1:T(8,128)(2,1)S(1)}, u32[]{:S(2)}, u32[]{:S(2)}) %collective-permute-start.8) | collective-permute-done | bytes 1048608 | tf_op jit(solution)/shard_map/ppermute | solution.py:26
  319.7 3.9 copy.130
  323.6 3.0 fusion.52
  326.6 214.7 %while.13 = (s32[]{:T(128)}, f32[256,2048]{1,0:T(8,128)S(1)}, f32[8,256,2048]{2,1,0:T(8,128)}, f32[8,256,32]{1,2,0:T(8,128)}, bf16[8,256,256]{2,1,0:T(8,128)(2,1...) while((s32[]{:T(128)}, f32[256,2048]{1,0:T(8,128)S(1)}, ...), condition=%wide.region_3.4_spmd.clone, body=%wide.region_0.3_spmd.clone.sunk | while | flops 857301120 | bytes 35264520 | solution.py:94
  334.3 4.2 fusion.75
  338.5 2.9 copy.182
  345.8 4.1 fusion.76
  361.2 4.2 fusion.75
  372.7 4.0 fusion.76
  388.0 4.2 fusion.75
  399.5 4.1 fusion.76
  414.9 4.2 fusion.75
  426.3 4.1 fusion.76
  441.7 4.2 fusion.75
  453.2 4.1 fusion.76
  468.6 4.2 fusion.75
  480.1 4.0 fusion.76
  495.4 4.2 fusion.75
  506.9 4.0 fusion.76
  522.3 4.2 fusion.75
  533.7 4.0 fusion.76
  541.4 3.8 collective-permute-start.9
  546.4 9.1 %reduce-window.16 = f32[32,16,128]{2,1,0:T(8,128)S(1)} reduce-window(f32[32,16,128]{2,1,0:T(8,128)S(1)} %bitcast.191, f32[]{:T(128)} %constant.34.clone.1), window={size=1x1x128 pad=0_0x0_0x127_0}, to_apply=%region_4.5 | reduce-window | flops 8323072 | bytes 524292 | tf_op jit(solution)/shard_map/reduce-window.2
  556.6 11.5 %collective-permute-done.9 = f32[256,2048]{1,0:T(8,128)} collective-permute-done((f32[256,2048]{1,0:T(8,128)S(1)}, f32[256,2048]{1,0:T(8,128)}, u32[]{:S(2)}, u32[]{:S(2)}) %collective-permute-start.9) | collective-permute-done | bytes 2097184 | tf_op jit(solution)/shard_map/ppermute | solution.py:34
  570.1 4.7 collective-permute-start.10
  574.8 22.7 %collective-permute-done.10 = f32[256,2048]{1,0:T(8,128)S(1)} collective-permute-done((f32[256,2048]{1,0:T(8,128)S(1)}, f32[256,2048]{1,0:T(8,128)S(1)}, u32[]{:S(2)}, u32[]{:S(2)}) %collective-permute-start.10) | collective-permute-done | bytes 2097184 | tf_op jit(solution)/shard_map/ppermute | solution.py:34
  598.9 4.4 collective-permute-start.11
  603.6 7.9 %broadcast_in_dim.92 = f32[2048,32,64]{0,2,1:T(8,128)} broadcast(f32[2048,32]{0,1:T(8,128)S(1)} %fusion.50), dimensions={0,1} | broadcast | bytes 17039360 | tf_op jit(solution)/shard_map/broadcast_in_dim | solution.py:49
  611.5 17.8 %copy.145 = f32[2048,2048]{1,0:T(8,128)} copy(f32[2048,2048]{0,1:T(8,128)} %bitcast.181) | data formatting | bytes 33554432 | tf_op jit(solution)/shard_map/reshape | solution.py:49
  629.3 18.7 %fusion.31 = bf16[2048,2048]{1,0:T(8,128)(2,1)} fusion(f32[8,256,2048]{2,1,0:T(8,128)} %get-tuple-element.48, f32[2048,2048]{1,0:T(8,128)} %copy.145, bf16[2048,1,2048]{2,0,1:T(8,128)(2,1)} %constant_dynamic-update-slice_fusion, f32[2048]{0:T(1024)S(1)} %mul.240, bf16[256,2048]{1,0:T(8,128)(2,1)} %collective-permute-done.11, bf16[2048,512]{1,0:T(8,128)(2,1)S(1)} %bitcast.185), kind=kOutput, calls=%fused_computation.53 | convolution fusion | flops 2172649472 | bytes 52436992 | tf_op jit(solution)/shard_map/dot_general | solution.py:156
  (248 shorter events, 203.6 us)
Async XLA Ops:
  1.7 54.2 %collective-permute-start.1 = (bf16[3,16384]{1,0:T(4,128)(2,1)}, bf16[3,16384]{1,0:T(4,128)(2,1)}, u32[]{:S(2)}, u32[]{:S(2)}) collective-permute-start(bf16[3,16384]{1,0:T(4,128)(2,1)} %slice.90), channel_id=1, source_target_pairs={{0,1},{1,2},{2,3},{3,4},{4,5},{5,6},{6,7},{7,8},{8,9},{9,10},{10,1... | collective-permute-start | bytes 294920 | tf_op jit(solution)/shard_map/ppermute | solution.py:34
  6.5 68.4 %all-to-all-start = ((bf16[256,8,32]{0,2,1:T(8,128)(2,1)}), bf16[256,8,32]{0,2,1:T(8,128)(2,1)S(1)}, u32[]{:S(2)}, u32[]{:S(2)}) async-start(bf16[256,8,32]{0,2,1:T(8,128)(2,1)} %bitcast), calls=%async_computation | async-start | bytes 262144 | tf_op jit(solution)/shard_map/all_to_all | solution.py:136
  13.1 22.8 %collective-permute-start = (bf16[3,4096]{1,0:T(4,128)(2,1)S(1)}, bf16[3,4096]{1,0:T(4,128)(2,1)}, u32[]{:S(2)}, u32[]{:S(2)}) collective-permute-start(bf16[3,4096]{1,0:T(4,128)(2,1)S(1)} %slice.80), channel_id=1, source_target_pairs={{0,1},{1,2},{2,3},{3,4},{4,5},{5,6},{6,7},{7,8},{8,9},{9,10},{10,1... | collective-permute-start | bytes 73736 | tf_op jit(solution)/shard_map/ppermute | solution.py:34
  37.1 1.4 copy-start.3
  37.2 1.4 copy-start.4
  37.2 1.4 copy-start.5
  37.2 1.4 copy-start.7
  45.5 4.8 copy-start.8
  60.0 20.0 %copy-start.6 = (f32[16384]{0:T(1024)S(1)}, f32[16384]{0:T(1024)}, u32[]{:S(2)}) copy-start(f32[16384]{0:T(1024)} %param.20) | copy-start | bytes 196612
  74.8 76.2 %copy-start.2 = (bf16[256,8,32]{0,2,1:T(8,128)(2,1)}, bf16[256,8,32]{0,2,1:T(8,128)(2,1)S(1)}, u32[]{:S(2)}) copy-start(bf16[256,8,32]{0,2,1:T(8,128)(2,1)S(1)} %all-to-all-done) | copy-start | bytes 393220
  74.8 244.8 %all-to-all-start.1 = ((bf16[256,8,512]{0,2,1:T(8,128)(2,1)}), bf16[256,8,512]{0,2,1:T(8,128)(2,1)}, u32[]{:S(2)}, u32[]{:S(2)}) async-start(bf16[256,8,512]{0,2,1:T(8,128)(2,1)} %bitcast.10), calls=%async_computation.1 | async-start | bytes 4194304 | tf_op jit(solution)/shard_map/all_to_all | solution.py:135
  123.7 7.8 %copy-start.9 = (f32[256]{0:T(256)S(1)}, f32[256]{0:T(256)}, u32[]{:S(2)}) copy-start(f32[256]{0:T(256)} %param.17) | copy-start | bytes 3076
  123.7 7.9 %copy-start.10 = (f32[256]{0:T(256)S(1)}, f32[256]{0:T(256)}, u32[]{:S(2)}) copy-start(f32[256]{0:T(256)} %param.16) | copy-start | bytes 3076
  126.0 26.0 %collective-permute-start.2 = (bf16[256,1,2048]{2,0,1:T(8,128)(2,1)}, bf16[256,1,2048]{2,0,1:T(8,128)(2,1)}, u32[]{:S(2)}, u32[]{:S(2)}) collective-permute-start(bf16[256,1,2048]{2,0,1:T(8,128)(2,1)} %copy.149), channel_id=1, source_target_pairs={{0,1},{1,0},{2,3},{3,2},{4,5},{5,4},{6,7},{7,6},{8,9},{9,8},{10,11... | collective-permute-start | bytes 3145736 | tf_op jit(solution)/shard_map/ppermute | solution.py:26
  128.6 59.3 %collective-permute-start.3 = (bf16[256,1,2048]{2,0,1:T(8,128)(2,1)}, bf16[256,1,2048]{2,0,1:T(8,128)(2,1)}, u32[]{:S(2)}, u32[]{:S(2)}) collective-permute-start(bf16[256,1,2048]{2,0,1:T(8,128)(2,1)} %copy.150), channel_id=1, source_target_pairs={{0,2},{1,3},{2,0},{3,1},{4,6},{5,7},{6,4},{7,5},{8,10},{9,11},{10,... | collective-permute-start | bytes 3145736 | tf_op jit(solution)/shard_map/ppermute | solution.py:26
  131.3 79.2 %collective-permute-start.4 = (bf16[256,1,2048]{2,0,1:T(8,128)(2,1)}, bf16[256,1,2048]{2,0,1:T(8,128)(2,1)}, u32[]{:S(2)}, u32[]{:S(2)}) collective-permute-start(bf16[256,1,2048]{2,0,1:T(8,128)(2,1)} %copy.151), channel_id=1, source_target_pairs={{0,3},{1,2},{2,1},{3,0},{4,7},{5,6},{6,5},{7,4},{8,11},{9,10},{10,... | collective-permute-start | bytes 3145736 | tf_op jit(solution)/shard_map/ppermute | solution.py:26
  136.3 76.5 %collective-permute-start.5 = (bf16[256,1,2048]{2,0,1:T(8,128)(2,1)}, bf16[256,1,2048]{2,0,1:T(8,128)(2,1)}, u32[]{:S(2)}, u32[]{:S(2)}) collective-permute-start(bf16[256,1,2048]{2,0,1:T(8,128)(2,1)} %copy.152), channel_id=1, source_target_pairs={{0,4},{1,5},{2,6},{3,7},{4,0},{5,1},{6,2},{7,3},{8,12},{9,13},{10,... | collective-permute-start | bytes 3145736 | tf_op jit(solution)/shard_map/ppermute | solution.py:26
  138.6 7.7 %copy-start.1 = (bf16[256,1,2048]{2,0,1:T(8,128)(2,1)S(1)}, bf16[256,1,2048]{2,0,1:T(8,128)(2,1)}, u32[]{:S(2)}) copy-start(bf16[256,1,2048]{2,0,1:T(8,128)(2,1)} %copy.148) | copy-start | bytes 3145732
  138.6 131.3 %collective-permute-start.6 = (bf16[256,1,2048]{2,0,1:T(8,128)(2,1)}, bf16[256,1,2048]{2,0,1:T(8,128)(2,1)}, u32[]{:S(2)}, u32[]{:S(2)}) collective-permute-start(bf16[256,1,2048]{2,0,1:T(8,128)(2,1)} %copy.153), channel_id=1, source_target_pairs={{0,5},{1,4},{2,7},{3,6},{4,1},{5,0},{6,3},{7,2},{8,13},{9,12},{10,... | collective-permute-start | bytes 3145736 | tf_op jit(solution)/shard_map/ppermute | solution.py:26
  152.1 143.2 %collective-permute-start.7 = (bf16[256,1,2048]{2,0,1:T(8,128)(2,1)}, bf16[256,1,2048]{2,0,1:T(8,128)(2,1)S(1)}, u32[]{:S(2)}, u32[]{:S(2)}) collective-permute-start(bf16[256,1,2048]{2,0,1:T(8,128)(2,1)} %copy.154), channel_id=1, source_target_pairs={{0,6},{1,7},{2,4},{3,5},{4,2},{5,3},{6,0},{7,1},{8,14},{9,15},{10,... | collective-permute-start | bytes 3145736 | tf_op jit(solution)/shard_map/ppermute | solution.py:26
  188.0 130.7 %collective-permute-start.8 = (bf16[256,1,2048]{2,0,1:T(8,128)(2,1)}, bf16[256,1,2048]{2,0,1:T(8,128)(2,1)S(1)}, u32[]{:S(2)}, u32[]{:S(2)}) collective-permute-start(bf16[256,1,2048]{2,0,1:T(8,128)(2,1)} %copy.155), channel_id=1, source_target_pairs={{0,7},{1,6},{2,5},{3,4},{4,3},{5,2},{6,1},{7,0},{8,15},{9,14},{10,... | collective-permute-start | bytes 3145736 | tf_op jit(solution)/shard_map/ppermute | solution.py:26
  541.4 26.8 %collective-permute-start.9 = (f32[256,2048]{1,0:T(8,128)S(1)}, f32[256,2048]{1,0:T(8,128)}, u32[]{:S(2)}, u32[]{:S(2)}) collective-permute-start(f32[256,2048]{1,0:T(8,128)S(1)} %get-tuple-element.49), channel_id=1, source_target_pairs={{0,8},{8,16},{16,24},{1,9},{9,17},{17,25},{2,10},{10,18},{18,26},{... | collective-permute-start | bytes 6291464 | tf_op jit(solution)/shard_map/ppermute | solution.py:34
  556.1 47.2 %copy-start.11 = (f32[256]{0:T(256)S(1)}, f32[256]{0:T(256)}, u32[]{:S(2)}) copy-start(f32[256]{0:T(256)} %param.18) | copy-start | bytes 3076
  570.1 27.5 %collective-permute-start.10 = (f32[256,2048]{1,0:T(8,128)S(1)}, f32[256,2048]{1,0:T(8,128)S(1)}, u32[]{:S(2)}, u32[]{:S(2)}) collective-permute-start(f32[256,2048]{1,0:T(8,128)S(1)} %multiply_add_fusion.1), channel_id=1, source_target_pairs={{0,8},{8,16},{16,24},{1,9},{9,17},{17,25},{2,10},{10,18},{18,26},{... | collective-permute-start | bytes 6291464 | tf_op jit(solution)/shard_map/ppermute | solution.py:34
  598.9 30.4 %collective-permute-start.11 = (bf16[256,2048]{1,0:T(8,128)(2,1)}, bf16[256,2048]{1,0:T(8,128)(2,1)}, u32[]{:S(2)}, u32[]{:S(2)}) collective-permute-start(bf16[256,2048]{1,0:T(8,128)(2,1)} %multiply_add_fusion), channel_id=1, source_target_pairs={{0,8},{8,16},{16,24},{1,9},{9,17},{17,25},{2,10},{10,18},{18,26},{... | collective-permute-start | bytes 3145736 | tf_op jit(solution)/shard_map/ppermute | solution.py:34
  611.5 17.8 %copy-start = (bf16[8,256,1,512]{3,1,0,2:T(8,128)(2,1)S(1)}, bf16[8,256,1,512]{3,1,0,2:T(8,128)(2,1)}, u32[]{:S(2)}) copy-start(bf16[8,256,1,512]{3,1,0,2:T(8,128)(2,1)} %copy.130) | copy-start | bytes 6291460
